TPU v7x, 128 devices: a whole 4x4x4 slice. The times are simulated.
128 devices in a mesh: rows: 8 (over z, core), seq: 16 (over x, y).
Axes of the slice: x: 4, y: 4, z: 4, core: 2. Of those that a mesh axis runs over, the one named last changes fastest.
Arguments:
- queries: bfloat16 [4096, 4096], P('seq'), may hold values from -50 to 50
- keys: bfloat16 [4096, 4096], P('seq'), may hold values from -6 to 6
- values: bfloat16 [4096, 4096], P('seq'), may hold values from -6 to 6
- grad_out: bfloat16 [8, 4096, 4096], P('rows', 'seq'), may hold values from -6 to 6
- table: bfloat16 [33, 4096], replicated, may hold values from -6 to 6
- positions: int32 [8], P('rows'), may hold values from 0 to 4095
- residues: int32 [8], P('rows'), may hold values from 4 to 23
- tiles: int32 [32, 8], replicated, may hold values from 0 to 31, as said below
- counts: int32 [32], replicated, may hold values from 1 to 8, as said below
Outputs:
- grad_queries: bfloat16 [8, 4096, 4096], P('rows', 'seq')
- grad_keys: bfloat16 [8, 4096, 4096], P('rows', 'seq')
- grad_values: bfloat16 [8, 4096, 4096], P('rows', 'seq')
Inputs may be any that keep to these rules, and one draw needn't show every extreme that they name: `tiles`: row i lists key blocks: entry 0 is i itself, the others differ from i and from each other. Only the first counts[i] entries of row i of tiles are used; some query block uses all 8.
All inputs are finite; a program needn't handle non-finite values.
Results may differ from a plain program's by a relative error of at most 0.0085.
Values may be sent and summed in bfloat16 or wider, within the bound.
No kernel may reach another device: no remote copies, remote signals or barrier semaphores. Data moves between devices by JAX's collectives and lax.ppermute only.
A program may use at most 128 MiB of HBM per device.

v0:
```python
import functools
import math

import jax
import jax.numpy as jnp
from jax import lax
from jax.experimental import pallas as pl
from jax.experimental.pallas import tpu as pltpu
from jax.sharding import PartitionSpec as P

D_HEAD = 128
BLOCK = 128
TILES = 8
HEADS_LOCAL = 2
SCALE = D_HEAD ** (-0.5)
EXP_SCALE = SCALE * math.log2(math.e)


def pack_first(share, queries, keys, values, row_devices, seq_devices):
    toks, width = queries.shape
    rows = toks // row_devices
    wide = HEADS_LOCAL * D_HEAD

    def body(share_ref, *refs):
        out_ref = refs[-1]
        for n, ref in enumerate(refs[:-1]):
            for dest in range(seq_devices):
                start = dest * wide
                out_ref[dest, n * rows : (n + 1) * rows] = ref[:, start : start + D_HEAD]

    near = pl.BlockSpec((rows, width), lambda g, share_ref: (share_ref[0], 0))
    out_dims = (seq_devices, 3 * rows, D_HEAD)
    return pl.pallas_call(
        body,
        grid_spec=pltpu.PrefetchScalarGridSpec(
            num_scalar_prefetch=1,
            grid=(1,),
            in_specs=[near, near, near],
            out_specs=pl.BlockSpec(out_dims, lambda g, share_ref: (0, 0, 0)),
        ),
        out_shape=jax.ShapeDtypeStruct(out_dims, jnp.bfloat16),
        name="pack_first",
    )(share, queries, keys, values)


def pack_rest(numbers, queries, keys, values, grad_out, table, row_devices, seq_devices):
    toks, width = grad_out.shape
    rows = toks // row_devices
    wide = HEADS_LOCAL * D_HEAD
    bases = (0, 6 * rows)

    def body(numbers_ref, *refs):
        share_refs = refs[:6]
        g_ref, table_ref = refs[6:8]
        outs = refs[8:]
        local = numbers_ref[2]
        residue = numbers_ref[3]
        for dest in range(seq_devices):
            for n, ref in enumerate(share_refs):
                start = dest * wide + D_HEAD
                outs[1][dest, n * rows : (n + 1) * rows] = ref[:, start : start + D_HEAD]
            for head in range(HEADS_LOCAL):
                start = dest * wide + head * D_HEAD
                outs[head][dest, bases[head] : bases[head] + toks] = g_ref[
                    :, start : start + D_HEAD
                ]

        @pl.when(jnp.logical_and(local >= 0, local < toks))
        def _():
            base = pl.multiple_of((local // 16) * 16, 16)
            picks = lax.broadcasted_iota(jnp.int32, (table.shape[0], D_HEAD), 0) == residue
            here = lax.broadcasted_iota(jnp.int32, (16, D_HEAD), 0) == local - base
            for dest in range(seq_devices):
                for head in range(HEADS_LOCAL):
                    start = dest * wide + head * D_HEAD
                    picked = table_ref[:, start : start + D_HEAD].astype(jnp.float32)
                    added = jnp.sum(jnp.where(picks, picked, 0.0), axis=0, keepdims=True)
                    now = g_ref[pl.ds(base, 16), start : start + D_HEAD].astype(jnp.float32)
                    outs[head][dest, pl.ds(pl.multiple_of(bases[head] + base, 16), 16), :] = (
                        now + jnp.where(here, added, 0.0)
                    ).astype(jnp.bfloat16)

    near = pl.BlockSpec((rows, width), lambda g, numbers_ref: (numbers_ref[0], 0))
    far = pl.BlockSpec((rows, width), lambda g, numbers_ref: (numbers_ref[1], 0))
    dims = [(seq_devices, base + toks, D_HEAD) for base in bases]
    return pl.pallas_call(
        body,
        grid_spec=pltpu.PrefetchScalarGridSpec(
            num_scalar_prefetch=1,
            grid=(1,),
            in_specs=[near, near, near, far, far, far]
            + [
                pl.BlockSpec((toks, width), lambda g, s: (0, 0)),
                pl.BlockSpec(table.shape, lambda g, s: (0, 0)),
            ],
            out_specs=[pl.BlockSpec(d, lambda g, s: (0, 0, 0)) for d in dims],
        ),
        out_shape=[jax.ShapeDtypeStruct(d, jnp.bfloat16) for d in dims],
        cost_estimate=pl.CostEstimate(
            flops=5_000_000_000, transcendentals=0, bytes_accessed=4 * toks * width
        ),
        name="pack_rest",
    )(numbers, queries, keys, values, queries, keys, values, grad_out, table)


def dot_nt(left, right):
    return lax.dot_general(left, right, (((1,), (1,)), ((), ())), preferred_element_type=jnp.float32)


def dot_nn(left, right):
    return lax.dot_general(left, right, (((1,), (0,)), ((), ())), preferred_element_type=jnp.float32)


def attention(head, tiles, counts, order, sources, arrays, parts, cot, toks, row_devices):
    seq_devices = arrays[0].shape[0]
    rows = toks // row_devices
    block_count = seq_devices * toks // BLOCK
    per_dev = toks // BLOCK
    quarters = BLOCK // rows
    n_arrays = len(arrays)
    n_in = 1 + 3 * len(parts)
    many = 4

    def body(tiles_ref, counts_ref, order_ref, source_ref, *refs):
        array_refs = refs[:n_arrays]
        out_hbm = refs[n_arrays]
        q_v, kv_v, c_v, kt_v, grads_v, out_ref, even_s, odd_s, even_t, odd_t, sem = refs[
            n_arrays + 1 :
        ]
        found_v, terms_v = (even_s, odd_s), (even_t, odd_t)
        lanes = (None, pl.ds(0, D_HEAD), pl.ds(D_HEAD, D_HEAD))
        copies = []
        for p, (which_array, begin_row, devs) in enumerate(parts):
            share = source_ref[p]
            for which in range(3):
                if which == 0:
                    dst = q_v.at[pl.ds(*devs), share // quarters, share % quarters]
                else:
                    dst = kv_v.at[
                        pl.ds(*devs), share // quarters, share % quarters, :, lanes[which]
                    ]
                src = array_refs[which_array].at[:, pl.ds(begin_row + which * rows, rows)]
                copies.append(pltpu.make_async_copy(src, dst, sem.at[3 * p + which]))
        copies.append(
            pltpu.make_async_copy(
                array_refs[cot[0]].at[:, pl.ds(cot[1], toks)], c_v, sem.at[n_in - 1]
            )
        )
        for copy in copies:
            copy.start()

        def clear(b, carry):
            grads_v[b] = jnp.zeros((BLOCK, 2 * D_HEAD), jnp.float32)
            return carry

        for ref in found_v + terms_v:
            ref[...] = jnp.zeros(ref.shape, ref.dtype)

        lax.fori_loop(0, block_count, clear, 0)
        for copy in copies:
            copy.wait()

        def flip(g, carry):
            for n in range(many):
                b = g * many + n
                block = kv_v[b // per_dev, b % per_dev, :, :, :D_HEAD]
                kt_v[b] = block.reshape(BLOCK, D_HEAD).T
            return carry

        lax.fori_loop(0, block_count // many, flip, 0)

        def at_block(b):
            return pl.ds(pl.multiple_of((b % per_dev) * BLOCK, BLOCK), BLOCK)

        def tile_of(i, j):
            return jnp.where(j < counts_ref[i], tiles_ref[i * TILES + j], i)

        def begin(i, count, found_ref):
            q_b = q_v[i // per_dev, i % per_dev].reshape(BLOCK, D_HEAD)
            c_b = c_v[i // per_dev, at_block(i), :]
            ids = [tile_of(i, j) for j in range(count)]
            blocks = [kv_v[t // per_dev, t % per_dev] for t in ids]
            k_all = jnp.concatenate(
                [x[:, :, :D_HEAD].reshape(BLOCK, D_HEAD) for x in blocks], axis=0
            )
            v_all = jnp.concatenate(
                [x[:, :, D_HEAD:].reshape(BLOCK, D_HEAD) for x in blocks], axis=0
            )
            found_ref[: count * BLOCK, :D_HEAD] = dot_nt(k_all, q_b)
            found_ref[: count * BLOCK, D_HEAD:] = dot_nt(v_all, c_b)

        def middle(used, count, found_ref, terms_ref):
            cuts = [slice(j * BLOCK, (j + 1) * BLOCK) for j in range(count)]
            tops = [
                jnp.where(j < used, jnp.max(found_ref[c, :D_HEAD], axis=0, keepdims=True), -jnp.inf)
                for j, c in enumerate(cuts)
            ]
            top = functools.reduce(jnp.maximum, tops) * EXP_SCALE
            total, delta, probs = 0.0, 0.0, []
            for j, c in enumerate(cuts):
                shift = jnp.where(j < used, top, jnp.inf)
                p = jnp.exp2(found_ref[c, :D_HEAD] * EXP_SCALE - shift)
                total = total + p
                delta = delta + p * found_ref[c, D_HEAD:]
                probs.append(p)
            total = jnp.sum(total, axis=0, keepdims=True)
            inverse = jnp.where(used > 0, 1.0 / total, 0.0)
            delta = jnp.sum(delta, axis=0, keepdims=True) * inverse
            for c, p in zip(cuts, probs):
                p = p * inverse
                terms_ref[c, :D_HEAD] = (p * (found_ref[c, D_HEAD:] - delta)).astype(jnp.bfloat16)
                terms_ref[c, D_HEAD:] = p.astype(jnp.bfloat16)

        def end(i, count, terms_ref):
            q_b = q_v[i // per_dev, i % per_dev].reshape(BLOCK, D_HEAD)
            c_b = c_v[i // per_dev, at_block(i), :]
            ids = [tile_of(i, j) for j in range(count)]
            scores = terms_ref[: count * BLOCK, :D_HEAD]
            probs = terms_ref[: count * BLOCK, D_HEAD:]
            key_terms = dot_nn(scores, q_b)
            value_terms = dot_nn(probs, c_b)
            grad_q = dot_nn(jnp.concatenate([kt_v[t] for t in ids], axis=1), scores)
            for j, t in enumerate(ids):
                grads_v[t, :, :D_HEAD] += key_terms[j * BLOCK : (j + 1) * BLOCK]
                grads_v[t, :, D_HEAD:] += value_terms[j * BLOCK : (j + 1) * BLOCK]
            out_ref[i // per_dev, 0, at_block(i), :] = (grad_q.T * SCALE).astype(jnp.bfloat16)

        def step(half, carry):
            for parity in range(2):
                g = 2 * half + parity
                first = order_ref[jnp.minimum(g, block_count - 1)]
                second = order_ref[jnp.clip(g - 1, 0, block_count - 1)]
                third = order_ref[jnp.maximum(g - 2, 0)]
                used = jnp.where(g > 0, counts_ref[second], 0)
                most = counts_ref[third]

                def choose(low, high, first, second, third, used, most, parity):
                    if low == high:
                        end(third, low, terms_v[parity])
                        middle(used, low, found_v[1 - parity], terms_v[1 - parity])
                        begin(first, low, found_v[parity])
                        return
                    split = (low + high) // 2

                    @pl.when(most <= split)
                    def _():
                        choose(low, split, first, second, third, used, most, parity)

                    @pl.when(most > split)
                    def _():
                        choose(split + 1, high, first, second, third, used, most, parity)

                choose(1, TILES, first, second, third, used, most, parity)

            return carry

        lax.fori_loop(0, block_count // 2 + 1, step, 0)

        stored = [pltpu.make_async_copy(out_ref.at[:, 0], out_hbm.at[:, 0], sem.at[n_in])]
        stored[0].start()
        quarter = seq_devices // many
        for part in range(many):

            def finish(dev, carry):
                for n in range(per_dev):
                    grads = grads_v[dev * per_dev + n]
                    at = pl.ds(n * BLOCK, BLOCK)
                    out_ref[dev, 1, at, :] = (grads[:, :D_HEAD] * SCALE).astype(jnp.bfloat16)
                    out_ref[dev, 2, at, :] = grads[:, D_HEAD:].astype(jnp.bfloat16)
                return carry

            lax.fori_loop(part * quarter, (part + 1) * quarter, finish, 0)
            at = (pl.ds(part * quarter, quarter), pl.ds(1, 2))
            stored.append(
                pltpu.make_async_copy(out_ref.at[at], out_hbm.at[at], sem.at[n_in + 1 + part])
            )
            stored[-1].start()
        for copy in stored:
            copy.wait()

    token_dims = (seq_devices, per_dev, quarters, rows)
    out_dims = (seq_devices, 3, toks, D_HEAD)
    return pl.pallas_call(
        body,
        grid_spec=pltpu.PrefetchScalarGridSpec(
            num_scalar_prefetch=4,
            grid=(1,),
            in_specs=[pl.BlockSpec(memory_space=pl.ANY)] * n_arrays,
            out_specs=pl.BlockSpec(memory_space=pltpu.HBM),
            scratch_shapes=[
                pltpu.VMEM(token_dims + (D_HEAD,), jnp.bfloat16),
                pltpu.VMEM(token_dims + (2 * D_HEAD,), jnp.bfloat16),
                pltpu.VMEM((seq_devices, toks, D_HEAD), jnp.bfloat16),
                pltpu.VMEM((block_count, D_HEAD, BLOCK), jnp.bfloat16),
                pltpu.VMEM((block_count, BLOCK, 2 * D_HEAD), jnp.float32),
                pltpu.VMEM(out_dims, jnp.bfloat16),
                pltpu.VMEM((TILES * BLOCK, 2 * D_HEAD), jnp.float32),
                pltpu.VMEM((TILES * BLOCK, 2 * D_HEAD), jnp.float32),
                pltpu.VMEM((TILES * BLOCK, 2 * D_HEAD), jnp.bfloat16),
                pltpu.VMEM((TILES * BLOCK, 2 * D_HEAD), jnp.bfloat16),
                pltpu.SemaphoreType.DMA((n_in + 1 + many,)),
            ],
        ),
        out_shape=pltpu.HBM(out_dims, jnp.bfloat16),
        compiler_params=pltpu.CompilerParams(vmem_limit_bytes=32 << 20),
        cost_estimate=pl.CostEstimate(
            flops=(40_000_000_000, 1_000_000)[head], transcendentals=0, bytes_accessed=1 << 20
        ),
    )(tiles, counts, order, sources, *arrays)


def unpack(head, arrived, outs, seq_devices):
    toks = arrived.shape[2]
    wide = HEADS_LOCAL * D_HEAD
    dims = (toks, seq_devices * wide)

    def body(src, *refs):
        dsts = refs[-4:-1]
        sem = refs[-1]
        copies = []
        for which in range(3):
            for dev in range(seq_devices):
                copies.append(
                    pltpu.make_async_copy(
                        src.at[dev, which],
                        dsts[which].at[:, pl.ds(dev * wide + head * D_HEAD, D_HEAD)],
                        sem.at[which * seq_devices + dev],
                    )
                )
        for copy in copies:
            copy.start()
        for copy in copies:
            copy.wait()

    return pl.pallas_call(
        body,
        in_specs=[pl.BlockSpec(memory_space=pl.ANY if outs else pltpu.VMEM)]
        + [pl.BlockSpec(memory_space=pl.ANY)] * len(outs),
        out_specs=[pl.BlockSpec(memory_space=pl.ANY)] * 3,
        out_shape=[jax.ShapeDtypeStruct(dims, jnp.bfloat16)] * 3,
        scratch_shapes=[pltpu.SemaphoreType.DMA((3 * seq_devices,))],
        input_output_aliases={1 + n: n for n in range(len(outs))},
        compiler_params=pltpu.CompilerParams(vmem_limit_bytes=8 << 20),
    )(arrived, *outs)


def per_device(queries, keys, values, grad_out, table, positions, residues, tiles, counts):
    toks = queries.shape[0]
    row_devices = lax.axis_size("rows")
    seq_devices = lax.axis_size("seq")
    row = lax.axis_index("rows").astype(jnp.int32)
    first = lax.axis_index("seq").astype(jnp.int32) * toks
    chips = row_devices // 2
    spread = lambda x: lax.all_to_all(x, "seq", split_axis=0, concat_axis=0, tiled=True)

    def shift(x, hops):
        pairs = [
            (z * 2 + c, ((z + hops) % chips) * 2 + c) for z in range(chips) for c in range(2)
        ]
        return lax.ppermute(x, "rows", pairs)

    def swap(x):
        return lax.ppermute(x, "rows", [(n, n ^ 1) for n in range(row_devices)])

    half = row_devices // 2
    rows = toks // row_devices
    numbers = jnp.stack([row, (row + half) % row_devices, positions[0] - first, residues[0]])
    own = pack_first(row[None], queries, keys, values, row_devices, seq_devices)
    cot, late = pack_rest(
        numbers, queries, keys, values, grad_out[0], table, row_devices, seq_devices
    )
    own = spread(own)
    flip = row ^ 1
    sources = [
        [row, flip, row - 2, row + 2, row + half, flip - 2, flip + 2, flip + half],
        [row, row + half, flip, flip + half, row - 2, row + 2, flip - 2, flip + 2],
    ]
    sources = [jnp.stack(x) % row_devices for x in sources]
    everyone = (0, seq_devices)
    parts = [
        [(n, 0, everyone) for n in range(8)],
        [(0, 0, everyone), (0, 3 * rows, everyone), (1, 0, everyone), (1, 3 * rows, everyone)]
        + [(n, 0, everyone) for n in range(2, 6)],
    ]

    blocks = jnp.arange(counts.shape[0], dtype=jnp.int32)
    ahead_of = (counts[None, :] > counts[:, None]) | (
        (counts[None, :] == counts[:, None]) & (blocks[None, :] < blocks[:, None])
    )
    place = jnp.sum(ahead_of.astype(jnp.int32), axis=1)
    order = jnp.sum(jnp.where(place[None, :] == blocks[:, None], blocks[None, :], 0), axis=1)

    def gather(near):
        back, ahead = shift(near, 1), shift(near, -1)
        return [back, ahead, swap(back), swap(ahead)]

    def work(head, arrays, cot_at):
        return attention(
            head,
            tiles.reshape(-1),
            counts,
            order,
            sources[head],
            arrays,
            parts[head],
            cot_at,
            toks,
            row_devices,
        )

    own, cot, late = lax.optimization_barrier((own, cot, late))
    back, ahead = shift(own, 1), shift(own, -1)
    sides = [back, ahead, shift(back, 1)]
    arrays = [own, swap(own)] + sides
    arrays = arrays + [swap(x) for x in sides]
    cot = spread(cot)
    late = spread(late)
    grads = work(0, arrays + [cot], (8, 0))
    grads, late = lax.optimization_barrier((grads, late))
    first_out = spread(grads)
    arrays = [late, swap(late[:, : 6 * rows])] + gather(late[:, : 3 * rows])
    grads = work(1, arrays, (0, 6 * rows))
    outs = unpack(0, first_out, [], seq_devices)
    outs = unpack(1, spread(grads), outs, seq_devices)
    return tuple(x[None] for x in outs)


def solution(mesh):
    placed = (
        P("seq", None),
        P("seq", None),
        P("seq", None),
        P("rows", "seq", None),
        P(),
        P("rows"),
        P("rows"),
        P(),
        P(),
    )

    return jax.shard_map(
        per_device,
        mesh=mesh,
        in_specs=placed,
        out_specs=(P("rows", "seq", None), P("rows", "seq", None), P("rows", "seq", None)),
        check_vma=False,
    )
```

profile of v0, /device:TPU:2, one launch (start us, length us, event | category | flops | bytes accessed | tf_op | source)
XLA Modules:
  0.0 165.8 jit_solution(9878920585997465426)
XLA Ops:
  0.6 1.9 %pack_first.1 = bf16[16,96,128]{2,1,0:T(8,128)(2,1)} custom-call(s32[1]{0:T(128)} %bitcast.share_ref, bf16[256,4096]{1,0:T(8,128)(2,1)} %refs_3_.1, bf16[256,4096]{1,0:T(8,128)(2,1)} %refs_4_.1, bf16[256,4096]{1,0:T(8,128)(2,1)} %refs_5_.1), custom_call_target="tpu_custom_call" | custom-call | tf_op jit(solution)/shard_map/pack_first/pallas_call | solution.py:33
  2.6 7.5 %all-to-all-start = ((bf16[16,96,128]{2,1,0:T(8,128)(2,1)}), bf16[16,96,128]{2,1,0:T(8,128)(2,1)S(1)}, u32[]{:S(2)}, u32[]{:S(2)}) async-start(bf16[16,96,128]{2,1,0:T(8,128)(2,1)} %pack_first.1), calls=%async_computation | async-start | bytes 786432 | tf_op jit(solution)/shard_map/all_to_all | solution.py:354
  11.9 4.8 %pack_rest.1 = (bf16[16,256,128]{2,1,0:T(8,128)(2,1)}, bf16[16,448,128]{2,1,0:T(8,128)(2,1)}) custom-call(s32[4]{0:T(128)} %pad_add_fusion.numbers_ref, bf16[256,4096]{1,0:T(8,128)(2,1)} %refs_3_.1, bf16[256,4096]{1,0:T(8,128)(2,1)} %refs_4_.1, bf16[256,4096]{1,0:T(8,128)(2,1)} %refs_5_.1, bf16[256,4096]{1,0:T(8,128)(2,1)} %refs_3_.1, ...), custom_call_target="tpu_custom_call" | custom-call | flops 5000000000 | bytes 4194304 | tf_op jit(solution)/shard_map/pack_rest/pallas_call | solution.py:86
  16.8 1.2 all-to-all-done.refs_0_
  18.0 1.9 %collective-permute-start.1 = (bf16[16,96,128]{2,1,0:T(8,128)(2,1)S(1)}, bf16[16,96,128]{2,1,0:T(8,128)(2,1)}, u32[]{:S(2)}, u32[]{:S(2)}) collective-permute-start(bf16[16,96,128]{2,1,0:T(8,128)(2,1)S(1)} %all-to-all-done.refs_0_), channel_id=1, source_target_pairs={{0,32},{16,48},{32,64},{48,80},{64,96},{80,112},{96,0},{112,16},{1... | collective-permute-start | bytes 1179656 | tf_op jit(solution)/shard_map/ppermute | solution.py:360
  19.9 6.1 %all-to-all-start.1 = ((bf16[16,256,128]{2,1,0:T(8,128)(2,1)}), bf16[16,256,128]{2,1,0:T(8,128)(2,1)S(1)}, u32[]{:S(2)}, u32[]{:S(2)}) async-start(bf16[16,256,128]{2,1,0:T(8,128)(2,1)} %get-tuple-element.19), calls=%async_computation.1 | async-start | bytes 2097152 | tf_op jit(solution)/shard_map/all_to_all | solution.py:354
  26.0 2.1 %collective-permute-start.2 = (bf16[16,96,128]{2,1,0:T(8,128)(2,1)S(1)}, bf16[16,96,128]{2,1,0:T(8,128)(2,1)}, u32[]{:S(2)}, u32[]{:S(2)}) collective-permute-start(bf16[16,96,128]{2,1,0:T(8,128)(2,1)S(1)} %all-to-all-done.refs_0_), channel_id=1, source_target_pairs={{0,96},{16,112},{32,0},{48,16},{64,32},{80,48},{96,64},{112,80},{1... | collective-permute-start | bytes 1179656 | tf_op jit(solution)/shard_map/ppermute | solution.py:360
  28.1 1.6 collective-permute-done.1.refs_2_
  30.2 5.6 %collective-permute-done.2.refs_3_ = bf16[16,96,128]{2,1,0:T(8,128)(2,1)} collective-permute-done((bf16[16,96,128]{2,1,0:T(8,128)(2,1)S(1)}, bf16[16,96,128]{2,1,0:T(8,128)(2,1)}, u32[]{:S(2)}, u32[]{:S(2)}) %collective-permute-start.2) | collective-permute-done | bytes 393248 | tf_op jit(solution)/shard_map/ppermute | solution.py:360
  35.9 4.1 %collective-permute-done.3.refs_4_ = bf16[16,96,128]{2,1,0:T(8,128)(2,1)} collective-permute-done((bf16[16,96,128]{2,1,0:T(8,128)(2,1)}, bf16[16,96,128]{2,1,0:T(8,128)(2,1)}, u32[]{:S(2)}, u32[]{:S(2)}) %collective-permute-start.3) | collective-permute-done | bytes 393248 | tf_op jit(solution)/shard_map/ppermute | solution.py:360
  40.6 8.0 %all-to-all-start.2 = ((bf16[16,448,128]{2,1,0:T(8,128)(2,1)}), bf16[16,448,128]{2,1,0:T(8,128)(2,1)S(1)}, u32[]{:S(2)}, u32[]{:S(2)}) async-start(bf16[16,448,128]{2,1,0:T(8,128)(2,1)} %get-tuple-element.20), calls=%async_computation.2 | async-start | bytes 3670016 | tf_op jit(solution)/shard_map/all_to_all | solution.py:354
  48.7 21.1 %shard_map.112 = bf16[16,3,256,128]{3,2,1,0:T(8,128)(2,1)} custom-call(s32[256]{0:T(256)S(1)} %reshape.13.tiles_ref, s32[32]{0:T(128)S(1)} %copy-done, s32[32]{0:T(128)S(1)} %select_reduce_fusion.order_ref, s32[8]{0:T(128)S(1)} %and_select_fusion.source_ref, bf16[16,96,128]{2,1,0:T(8,128)(2,1)S(1)} %all-to-all-done.refs_0_, ...), custom_call_target="tpu_custom_call" | custom-call | flops 40000000000 | bytes 1048576 | tf_op jit(solution)/shard_map/pallas_call | solution.py:283
  69.8 4.3 %all-to-all-done.2.refs_0_ = bf16[16,448,128]{2,1,0:T(8,128)(2,1)S(1)} async-done(((bf16[16,448,128]{2,1,0:T(8,128)(2,1)}), bf16[16,448,128]{2,1,0:T(8,128)(2,1)S(1)}, u32[]{:S(2)}, u32[]{:S(2)}) %all-to-all-start.2) | async-done | bytes 1835040 | tf_op jit(solution)/shard_map/all_to_all | solution.py:354
  74.1 7.1 %all-to-all-start.4 = ((bf16[16,3,256,128]{3,2,1,0:T(8,128)(2,1)}), bf16[16,3,256,128]{3,2,1,0:T(8,128)(2,1)}, u32[]{:S(2)}, u32[]{:S(2)}) async-start(bf16[16,3,256,128]{3,2,1,0:T(8,128)(2,1)} %shard_map.112), calls=%async_computation.4 | async-start | bytes 6291456 | tf_op jit(solution)/shard_map/all_to_all | solution.py:354
  81.5 1.8 %collective-permute-start.8 = (bf16[16,96,128]{2,1,0:T(8,128)(2,1)S(1)}, bf16[16,96,128]{2,1,0:T(8,128)(2,1)S(1)}, u32[]{:S(2)}, u32[]{:S(2)}) collective-permute-start(bf16[16,96,128]{2,1,0:T(8,128)(2,1)S(1)} %slice.7), channel_id=1, source_target_pairs={{0,32},{16,48},{32,64},{48,80},{64,96},{80,112},{96,0},{112,16},{1... | collective-permute-start | bytes 1179656 | tf_op jit(solution)/shard_map/ppermute | solution.py:360
  84.2 6.7 %collective-permute-done.9.refs_3_ = bf16[16,96,128]{2,1,0:T(8,128)(2,1)S(1)} collective-permute-done((bf16[16,96,128]{2,1,0:T(8,128)(2,1)S(1)}, bf16[16,96,128]{2,1,0:T(8,128)(2,1)S(1)}, u32[]{:S(2)}, u32[]{:S(2)}) %collective-permute-start.9) | collective-permute-done | bytes 393248 | tf_op jit(solution)/shard_map/ppermute | solution.py:360
  90.9 1.3 collective-permute-done.8.refs_2_
  92.8 1.3 collective-permute-done.10.refs_4_
  94.1 20.9 %shard_map.113 = bf16[16,3,256,128]{3,2,1,0:T(8,128)(2,1)} custom-call(s32[256]{0:T(256)S(1)} %reshape.13.tiles_ref, s32[32]{0:T(128)S(1)} %copy-done, s32[32]{0:T(128)S(1)} %select_reduce_fusion.order_ref, s32[8]{0:T(128)S(1)} %and_select_fusion.1.source_ref, bf16[16,448,128]{2,1,0:T(8,128)(2,1)S(1)} %all-to-all-done.2.refs_0_, ...), custom_call_target="tpu_custom_call" | custom-call | flops 1000000 | bytes 1048576 | tf_op jit(solution)/shard_map/pallas_call | solution.py:283
  115.0 5.1 %all-to-all-done.4.src = bf16[16,3,256,128]{3,2,1,0:T(8,128)(2,1)} async-done(((bf16[16,3,256,128]{3,2,1,0:T(8,128)(2,1)}), bf16[16,3,256,128]{3,2,1,0:T(8,128)(2,1)}, u32[]{:S(2)}, u32[]{:S(2)}) %all-to-all-start.4) | async-done | bytes 3145760 | tf_op jit(solution)/shard_map/all_to_all | solution.py:354
  120.1 7.3 %all-to-all-start.3 = ((bf16[16,3,256,128]{3,2,1,0:T(8,128)(2,1)}), bf16[16,3,256,128]{3,2,1,0:T(8,128)(2,1)S(1)}, u32[]{:S(2)}, u32[]{:S(2)}) async-start(bf16[16,3,256,128]{3,2,1,0:T(8,128)(2,1)} %shard_map.113), calls=%async_computation.3 | async-start | bytes 6291456 | tf_op jit(solution)/shard_map/all_to_all | solution.py:354
  127.4 3.9 %shard_map.114 = (bf16[256,4096]{1,0:T(8,128)(2,1)}, bf16[256,4096]{1,0:T(8,128)(2,1)}, bf16[256,4096]{1,0:T(8,128)(2,1)}) custom-call(bf16[16,3,256,128]{3,2,1,0:T(8,128)(2,1)} %all-to-all-done.4.src), custom_call_target="tpu_custom_call" | custom-call | tf_op jit(solution)/shard_map/pallas_call | solution.py:335
  131.4 32.2 %all-to-all-done.3.src = bf16[16,3,256,128]{3,2,1,0:T(8,128)(2,1)S(1)} async-done(((bf16[16,3,256,128]{3,2,1,0:T(8,128)(2,1)}), bf16[16,3,256,128]{3,2,1,0:T(8,128)(2,1)S(1)}, u32[]{:S(2)}, u32[]{:S(2)}) %all-to-all-start.3) | async-done | bytes 3145760 | tf_op jit(solution)/shard_map/all_to_all | solution.py:354
  163.5 2.0 %shard_map.115 = (bf16[256,4096]{1,0:T(8,128)(2,1)}, bf16[256,4096]{1,0:T(8,128)(2,1)}, bf16[256,4096]{1,0:T(8,128)(2,1)}) custom-call(bf16[16,3,256,128]{3,2,1,0:T(8,128)(2,1)S(1)} %all-to-all-done.3.src, bf16[256,4096]{1,0:T(8,128)(2,1)} %get-tuple-element.23.refs_0_, ...), custom_call_target="tpu_custom_call", output_to_operand_aliasing={{0}: (1, {}), {1}: (2, {}), {2}: (3, {})} | custom-call | tf_op jit(solution)/shard_map/pallas_call | solution.py:335
  (31 shorter events, 3.5 us)
Async XLA Ops:
  2.6 15.4 %all-to-all-start = ((bf16[16,96,128]{2,1,0:T(8,128)(2,1)}), bf16[16,96,128]{2,1,0:T(8,128)(2,1)S(1)}, u32[]{:S(2)}, u32[]{:S(2)}) async-start(bf16[16,96,128]{2,1,0:T(8,128)(2,1)} %pack_first.1), calls=%async_computation | async-start | bytes 786432 | tf_op jit(solution)/shard_map/all_to_all | solution.py:354
  16.8 23.2 %copy-start = (s32[32]{0:T(128)S(1)}, s32[32]{0:T(128)}, u32[]{:S(2)}) copy-start(s32[32]{0:T(128)} %counts_ref.3) | copy-start | bytes 388
  16.8 23.4 %copy-start.1 = (s32[32,8]{0,1:T(8,128)S(1)}, s32[32,8]{0,1:T(8,128)}, u32[]{:S(2)}) copy-start(s32[32,8]{0,1:T(8,128)} %param.16) | copy-start | bytes 3076
  18.0 11.7 %collective-permute-start.1 = (bf16[16,96,128]{2,1,0:T(8,128)(2,1)S(1)}, bf16[16,96,128]{2,1,0:T(8,128)(2,1)}, u32[]{:S(2)}, u32[]{:S(2)}) collective-permute-start(bf16[16,96,128]{2,1,0:T(8,128)(2,1)S(1)} %all-to-all-done.refs_0_), channel_id=1, source_target_pairs={{0,32},{16,48},{32,64},{48,80},{64,96},{80,112},{96,0},{112,16},{1... | collective-permute-start | bytes 1179656 | tf_op jit(solution)/shard_map/ppermute | solution.py:360
  19.9 20.7 %all-to-all-start.1 = ((bf16[16,256,128]{2,1,0:T(8,128)(2,1)}), bf16[16,256,128]{2,1,0:T(8,128)(2,1)S(1)}, u32[]{:S(2)}, u32[]{:S(2)}) async-start(bf16[16,256,128]{2,1,0:T(8,128)(2,1)} %get-tuple-element.19), calls=%async_computation.1 | async-start | bytes 2097152 | tf_op jit(solution)/shard_map/all_to_all | solution.py:354
  26.0 9.9 %collective-permute-start.2 = (bf16[16,96,128]{2,1,0:T(8,128)(2,1)S(1)}, bf16[16,96,128]{2,1,0:T(8,128)(2,1)}, u32[]{:S(2)}, u32[]{:S(2)}) collective-permute-start(bf16[16,96,128]{2,1,0:T(8,128)(2,1)S(1)} %all-to-all-done.refs_0_), channel_id=1, source_target_pairs={{0,96},{16,112},{32,0},{48,16},{64,32},{80,48},{96,64},{112,80},{1... | collective-permute-start | bytes 1179656 | tf_op jit(solution)/shard_map/ppermute | solution.py:360
  29.7 10.3 %collective-permute-start.3 = (bf16[16,96,128]{2,1,0:T(8,128)(2,1)}, bf16[16,96,128]{2,1,0:T(8,128)(2,1)}, u32[]{:S(2)}, u32[]{:S(2)}) collective-permute-start(bf16[16,96,128]{2,1,0:T(8,128)(2,1)} %collective-permute-done.1.refs_2_), channel_id=1, source_target_pairs={{0,32},{16,48},{32,64},{48,80},{64,96},{80,112},{96,0},{112,16},{1... | collective-permute-start | bytes 1179656 | tf_op jit(solution)/shard_map/ppermute | solution.py:360
  29.7 18.9 %collective-permute-start = (bf16[16,96,128]{2,1,0:T(8,128)(2,1)S(1)}, bf16[16,96,128]{2,1,0:T(8,128)(2,1)}, u32[]{:S(2)}, u32[]{:S(2)}) collective-permute-start(bf16[16,96,128]{2,1,0:T(8,128)(2,1)S(1)} %all-to-all-done.refs_0_), channel_id=1, source_target_pairs={{0,16},{16,0},{32,48},{48,32},{64,80},{80,64},{96,112},{112,96},{1... | collective-permute-start | bytes 1179656 | tf_op jit(solution)/shard_map/ppermute | solution.py:363
  29.7 18.9 %collective-permute-start.4 = (bf16[16,96,128]{2,1,0:T(8,128)(2,1)}, bf16[16,96,128]{2,1,0:T(8,128)(2,1)}, u32[]{:S(2)}, u32[]{:S(2)}) collective-permute-start(bf16[16,96,128]{2,1,0:T(8,128)(2,1)} %collective-permute-done.1.refs_2_), channel_id=1, source_target_pairs={{0,16},{16,0},{32,48},{48,32},{64,80},{80,64},{96,112},{112,96},{1... | collective-permute-start | bytes 1179656 | tf_op jit(solution)/shard_map/ppermute | solution.py:363
  35.9 12.8 %collective-permute-start.5 = (bf16[16,96,128]{2,1,0:T(8,128)(2,1)}, bf16[16,96,128]{2,1,0:T(8,128)(2,1)}, u32[]{:S(2)}, u32[]{:S(2)}) collective-permute-start(bf16[16,96,128]{2,1,0:T(8,128)(2,1)} %collective-permute-done.2.refs_3_), channel_id=1, source_target_pairs={{0,16},{16,0},{32,48},{48,32},{64,80},{80,64},{96,112},{112,96},{1... | collective-permute-start | bytes 1179656 | tf_op jit(solution)/shard_map/ppermute | solution.py:363
  40.0 8.7 %collective-permute-start.6 = (bf16[16,96,128]{2,1,0:T(8,128)(2,1)}, bf16[16,96,128]{2,1,0:T(8,128)(2,1)}, u32[]{:S(2)}, u32[]{:S(2)}) collective-permute-start(bf16[16,96,128]{2,1,0:T(8,128)(2,1)} %collective-permute-done.3.refs_4_), channel_id=1, source_target_pairs={{0,16},{16,0},{32,48},{48,32},{64,80},{80,64},{96,112},{112,96},{1... | collective-permute-start | bytes 1179656 | tf_op jit(solution)/shard_map/ppermute | solution.py:363
  40.6 33.5 %all-to-all-start.2 = ((bf16[16,448,128]{2,1,0:T(8,128)(2,1)}), bf16[16,448,128]{2,1,0:T(8,128)(2,1)S(1)}, u32[]{:S(2)}, u32[]{:S(2)}) async-start(bf16[16,448,128]{2,1,0:T(8,128)(2,1)} %get-tuple-element.20), calls=%async_computation.2 | async-start | bytes 3670016 | tf_op jit(solution)/shard_map/all_to_all | solution.py:354
  74.1 46.0 %all-to-all-start.4 = ((bf16[16,3,256,128]{3,2,1,0:T(8,128)(2,1)}), bf16[16,3,256,128]{3,2,1,0:T(8,128)(2,1)}, u32[]{:S(2)}, u32[]{:S(2)}) async-start(bf16[16,3,256,128]{3,2,1,0:T(8,128)(2,1)} %shard_map.112), calls=%async_computation.4 | async-start | bytes 6291456 | tf_op jit(solution)/shard_map/all_to_all | solution.py:354
  81.2 9.7 %collective-permute-start.9 = (bf16[16,96,128]{2,1,0:T(8,128)(2,1)S(1)}, bf16[16,96,128]{2,1,0:T(8,128)(2,1)S(1)}, u32[]{:S(2)}, u32[]{:S(2)}) collective-permute-start(bf16[16,96,128]{2,1,0:T(8,128)(2,1)S(1)} %slice.7), channel_id=1, source_target_pairs={{0,96},{16,112},{32,0},{48,16},{64,32},{80,48},{96,64},{112,80},{1... | collective-permute-start | bytes 1179656 | tf_op jit(solution)/shard_map/ppermute | solution.py:360
  81.5 10.7 %collective-permute-start.8 = (bf16[16,96,128]{2,1,0:T(8,128)(2,1)S(1)}, bf16[16,96,128]{2,1,0:T(8,128)(2,1)S(1)}, u32[]{:S(2)}, u32[]{:S(2)}) collective-permute-start(bf16[16,96,128]{2,1,0:T(8,128)(2,1)S(1)} %slice.7), channel_id=1, source_target_pairs={{0,32},{16,48},{32,64},{48,80},{64,96},{80,112},{96,0},{112,16},{1... | collective-permute-start | bytes 1179656 | tf_op jit(solution)/shard_map/ppermute | solution.py:360
  84.2 9.9 %collective-permute-start.7 = (bf16[16,192,128]{2,1,0:T(8,128)(2,1)}, bf16[16,192,128]{2,1,0:T(8,128)(2,1)S(1)}, u32[]{:S(2)}, u32[]{:S(2)}) collective-permute-start(bf16[16,192,128]{2,1,0:T(8,128)(2,1)} %slice.6), channel_id=1, source_target_pairs={{0,16},{16,0},{32,48},{48,32},{64,80},{80,64},{96,112},{112,96},{1... | collective-permute-start | bytes 2359304 | tf_op jit(solution)/shard_map/ppermute | solution.py:363
  90.9 1.9 %collective-permute-start.11 = (bf16[16,96,128]{2,1,0:T(8,128)(2,1)S(1)}, bf16[16,96,128]{2,1,0:T(8,128)(2,1)}, u32[]{:S(2)}, u32[]{:S(2)}) collective-permute-start(bf16[16,96,128]{2,1,0:T(8,128)(2,1)S(1)} %collective-permute-done.9.refs_3_), channel_id=1, source_target_pairs={{0,16},{16,0},{32,48},{48,32},{64,80},{80,64},{96,112},{112,96},{1... | collective-permute-start | bytes 1179656 | tf_op jit(solution)/shard_map/ppermute | solution.py:363
  92.2 1.9 %collective-permute-start.10 = (bf16[16,96,128]{2,1,0:T(8,128)(2,1)S(1)}, bf16[16,96,128]{2,1,0:T(8,128)(2,1)}, u32[]{:S(2)}, u32[]{:S(2)}) collective-permute-start(bf16[16,96,128]{2,1,0:T(8,128)(2,1)S(1)} %collective-permute-done.8.refs_2_), channel_id=1, source_target_pairs={{0,16},{16,0},{32,48},{48,32},{64,80},{80,64},{96,112},{112,96},{1... | collective-permute-start | bytes 1179656 | tf_op jit(solution)/shard_map/ppermute | solution.py:363
  120.1 43.4 %all-to-all-start.3 = ((bf16[16,3,256,128]{3,2,1,0:T(8,128)(2,1)}), bf16[16,3,256,128]{3,2,1,0:T(8,128)(2,1)S(1)}, u32[]{:S(2)}, u32[]{:S(2)}) async-start(bf16[16,3,256,128]{3,2,1,0:T(8,128)(2,1)} %shard_map.113), calls=%async_computation.3 | async-start | bytes 6291456 | tf_op jit(solution)/shard_map/all_to_all | solution.py:354
where the time goes:
time: 168 us; the launch traced here: 166 us
  waiting for transfers between devices  63.9 us (38%)
  Pallas kernels  54.7 us (33%)
  starting transfers between devices  42.7 us (25%)
  between operations  2.2 us (1%)
    all_to_all x5, waiting for transfers between devices, per_device(): lax.all_to_all(x, 'seq', split_axis=0, concat_axis=0, tiled=True)  42.8 us
    pallas_call x2, Pallas kernels, attention(): pl.pallas_call(body, grid_spec=pltpu.PrefetchScalarGridSpec(num_scalar_pr...  42 us
    all_to_all x5, starting transfers between devices, per_device(): lax.all_to_all(x, 'seq', split_axis=0, concat_axis=0, tiled=True)  36 us
    ppermute x5, waiting for transfers between devices, shift(): return lax.ppermute(x, 'rows', pairs)  19.3 us
    ppermute x5, starting transfers between devices, shift(): return lax.ppermute(x, 'rows', pairs)  6.16 us
    pallas_call x2, Pallas kernels, unpack(): pl.pallas_call(body, in_specs=[pl.BlockSpec(memory_space=pl.ANY if outs e...  5.98 us
    pallas_call x1, Pallas kernels, pack_rest(): pl.pallas_call(body, grid_spec=pltpu.PrefetchScalarGridSpec(num_scalar_pr...  4.83 us
  transfers between devices with their start and end apart: 17, of which 11 were waited for; matrix products, arithmetic and copies ran while one was open for 1% of the time, Pallas kernels for 31%

commit v1 on v0

--- a/solution.py
+++ b/solution.py
@@ -372,13 +372,15 @@
     own = spread(own)
     flip = row ^ 1
     sources = [
-        [row, flip, row - 2, row + 2, row + half, flip - 2, flip + 2, flip + half],
+        [row, flip, row - 2, row + 2, flip - 2, flip + 2] + [row + half] * 2 + [flip + half] * 2,
         [row, row + half, flip, flip + half, row - 2, row + 2, flip - 2, flip + 2],
     ]
     sources = [jnp.stack(x) % row_devices for x in sources]
     everyone = (0, seq_devices)
+    lows, highs = (0, seq_devices // 2), (seq_devices // 2, seq_devices // 2)
     parts = [
-        [(n, 0, everyone) for n in range(8)],
+        [(n, 0, everyone) for n in range(6)]
+        + [(6, 0, lows), (7, 0, highs), (8, 0, lows), (9, 0, highs)],
         [(0, 0, everyone), (0, 3 * rows, everyone), (1, 0, everyone), (1, 3 * rows, everyone)]
         + [(n, 0, everyone) for n in range(2, 6)],
     ]
@@ -410,12 +412,13 @@
 
     own, cot, late = lax.optimization_barrier((own, cot, late))
     back, ahead = shift(own, 1), shift(own, -1)
-    sides = [back, ahead, shift(back, 1)]
-    arrays = [own, swap(own)] + sides
-    arrays = arrays + [swap(x) for x in sides]
+    arrays = [own, swap(own), back, ahead]
+    arrays = arrays + [swap(back), swap(ahead)]
+    far = [shift(back[: seq_devices // 2], 1), shift(ahead[seq_devices // 2 :], -1)]
+    arrays = arrays + far + [swap(x) for x in far]
     cot = spread(cot)
     late = spread(late)
-    grads = work(0, arrays + [cot], (8, 0))
+    grads = work(0, arrays + [cot], (10, 0))
     grads, late = lax.optimization_barrier((grads, late))
     first_out = spread(grads)
     arrays = [late, swap(late[:, : 6 * rows])] + gather(late[:, : 3 * rows])

time: 168 us -> 175 us (1.042)
  starting transfers between devices: 42.7 us -> 46.3 us
  local copies, waits for them, and re-layouts: 1.31 us -> 3.19 us
    ppermute x5 -> x6, starting transfers between devices: 6.16 us -> 10.1 us  [shift(): return lax.ppermute(x, 'rows', pairs)]
    slice x0 -> x2, local copies, waits for them, and re-layouts: none -> 1.88 us  [the longest x1 0.94 us: per_device(): back[:seq_devices // 2]]
    ppermute x5 -> x6, waiting for transfers between devices: 19.3 us -> 21 us  [shift(): return lax.ppermute(x, 'rows', pairs)]
  transfers between devices with their start and end apart: 17 -> 19, of which waited for: 11 -> 11; matrix products, arithmetic and copies ran while one was open for 1% -> 2% of each run, Pallas kernels for 31% -> 29%
where the time goes in v1:
time: 175 us; the launch traced here: 173 us
  waiting for transfers between devices  65.1 us (37%)
  Pallas kernels  54.7 us (31%)
  starting transfers between devices  46.3 us (26%)
  local copies, waits for them, and re-layouts  3.19 us (2%)
  between operations  2.23 us (1%)
    all_to_all x5, waiting for transfers between devices, per_device(): lax.all_to_all(x, 'seq', split_axis=0, concat_axis=0, tiled=True)  42.4 us
    pallas_call x2, Pallas kernels, attention(): pl.pallas_call(body, grid_spec=pltpu.PrefetchScalarGridSpec(num_scalar_pr...  42 us
    all_to_all x5, starting transfers between devices, per_device(): lax.all_to_all(x, 'seq', split_axis=0, concat_axis=0, tiled=True)  35.6 us
    ppermute x6, waiting for transfers between devices, shift(): return lax.ppermute(x, 'rows', pairs)  21 us
    ppermute x6, starting transfers between devices, shift(): return lax.ppermute(x, 'rows', pairs)  10.1 us
    pallas_call x2, Pallas kernels, unpack(): pl.pallas_call(body, in_specs=[pl.BlockSpec(memory_space=pl.ANY if outs e...  5.98 us
    pallas_call x1, Pallas kernels, pack_rest(): pl.pallas_call(body, grid_spec=pltpu.PrefetchScalarGridSpec(num_scalar_pr...  4.83 us
  transfers between devices with their start and end apart: 19, of which 11 were waited for; matrix products, arithmetic and copies ran while one was open for 2% of the time, Pallas kernels for 29%

profile of v1, /device:TPU:2, one launch (start us, length us, event | category | flops | bytes accessed | tf_op | source)
XLA Modules:
  0.0 172.5 jit_solution(18380310775318127186)
XLA Ops:
  0.6 1.9 %pack_first.1 = bf16[16,96,128]{2,1,0:T(8,128)(2,1)} custom-call(s32[1]{0:T(128)} %bitcast.share_ref, bf16[256,4096]{1,0:T(8,128)(2,1)} %refs_3_.1, bf16[256,4096]{1,0:T(8,128)(2,1)} %refs_4_.1, bf16[256,4096]{1,0:T(8,128)(2,1)} %refs_5_.1), custom_call_target="tpu_custom_call" | custom-call | tf_op jit(solution)/shard_map/pack_first/pallas_call | solution.py:33
  2.6 7.5 %all-to-all-start = ((bf16[16,96,128]{2,1,0:T(8,128)(2,1)}), bf16[16,96,128]{2,1,0:T(8,128)(2,1)S(1)}, u32[]{:S(2)}, u32[]{:S(2)}) async-start(bf16[16,96,128]{2,1,0:T(8,128)(2,1)} %pack_first.1), calls=%async_computation | async-start | bytes 786432 | tf_op jit(solution)/shard_map/all_to_all | solution.py:354
  12.0 4.8 %pack_rest.1 = (bf16[16,256,128]{2,1,0:T(8,128)(2,1)}, bf16[16,448,128]{2,1,0:T(8,128)(2,1)}) custom-call(s32[4]{0:T(128)} %pad_add_fusion.numbers_ref, bf16[256,4096]{1,0:T(8,128)(2,1)} %refs_3_.1, bf16[256,4096]{1,0:T(8,128)(2,1)} %refs_4_.1, bf16[256,4096]{1,0:T(8,128)(2,1)} %refs_5_.1, bf16[256,4096]{1,0:T(8,128)(2,1)} %refs_3_.1, ...), custom_call_target="tpu_custom_call" | custom-call | flops 5000000000 | bytes 4194304 | tf_op jit(solution)/shard_map/pack_rest/pallas_call | solution.py:86
  16.8 1.1 all-to-all-done.refs_0_
  18.0 6.4 %all-to-all-start.1 = ((bf16[16,256,128]{2,1,0:T(8,128)(2,1)}), bf16[16,256,128]{2,1,0:T(8,128)(2,1)S(1)}, u32[]{:S(2)}, u32[]{:S(2)}) async-start(bf16[16,256,128]{2,1,0:T(8,128)(2,1)} %get-tuple-element.19), calls=%async_computation.1 | async-start | bytes 2097152 | tf_op jit(solution)/shard_map/all_to_all | solution.py:354
  24.3 3.9 %collective-permute-start.2 = (bf16[16,96,128]{2,1,0:T(8,128)(2,1)S(1)}, bf16[16,96,128]{2,1,0:T(8,128)(2,1)}, u32[]{:S(2)}, u32[]{:S(2)}) collective-permute-start(bf16[16,96,128]{2,1,0:T(8,128)(2,1)S(1)} %all-to-all-done.refs_0_), channel_id=1, source_target_pairs={{0,96},{16,112},{32,0},{48,16},{64,32},{80,48},{96,64},{112,80},{1... | collective-permute-start | bytes 1179656 | tf_op jit(solution)/shard_map/ppermute | solution.py:360
  28.2 7.2 %collective-permute-done.2.refs_3_ = bf16[16,96,128]{2,1,0:T(8,128)(2,1)} collective-permute-done((bf16[16,96,128]{2,1,0:T(8,128)(2,1)S(1)}, bf16[16,96,128]{2,1,0:T(8,128)(2,1)}, u32[]{:S(2)}, u32[]{:S(2)}) %collective-permute-start.2) | collective-permute-done | bytes 393248 | tf_op jit(solution)/shard_map/ppermute | solution.py:360
  36.4 3.9 %collective-permute-start.6 = (bf16[8,96,128]{2,1,0:T(8,128)(2,1)S(1)}, bf16[8,96,128]{2,1,0:T(8,128)(2,1)}, u32[]{:S(2)}, u32[]{:S(2)}) collective-permute-start(bf16[8,96,128]{2,1,0:T(8,128)(2,1)S(1)} %slice.17), channel_id=1, source_target_pairs={{0,96},{16,112},{32,0},{48,16},{64,32},{80,48},{96,64},{112,80},{1... | collective-permute-start | bytes 589832 | tf_op jit(solution)/shard_map/ppermute | solution.py:360
  42.5 1.0 collective-permute-done.6.refs_7_
  43.5 4.8 %collective-permute-done.5.refs_6_ = bf16[8,96,128]{2,1,0:T(8,128)(2,1)} collective-permute-done((bf16[8,96,128]{2,1,0:T(8,128)(2,1)S(1)}, bf16[8,96,128]{2,1,0:T(8,128)(2,1)}, u32[]{:S(2)}, u32[]{:S(2)}) %collective-permute-start.5) | collective-permute-done | bytes 196640 | tf_op jit(solution)/shard_map/ppermute | solution.py:360
  48.3 7.2 %all-to-all-start.2 = ((bf16[16,448,128]{2,1,0:T(8,128)(2,1)}), bf16[16,448,128]{2,1,0:T(8,128)(2,1)S(1)}, u32[]{:S(2)}, u32[]{:S(2)}) async-start(bf16[16,448,128]{2,1,0:T(8,128)(2,1)} %get-tuple-element.20), calls=%async_computation.2 | async-start | bytes 3670016 | tf_op jit(solution)/shard_map/all_to_all | solution.py:354
  55.6 21.1 %shard_map.112 = bf16[16,3,256,128]{3,2,1,0:T(8,128)(2,1)} custom-call(s32[256]{0:T(256)S(1)} %reshape.13.tiles_ref, s32[32]{0:T(128)S(1)} %copy-done, s32[32]{0:T(128)S(1)} %select_reduce_fusion.order_ref, s32[10]{0:T(128)S(1)} %and_select_fusion.source_ref, bf16[16,96,128]{2,1,0:T(8,128)(2,1)S(1)} %all-to-all-done.refs_0_, ...), custom_call_target="tpu_custom_call" | custom-call | flops 40000000000 | bytes 1048576 | tf_op jit(solution)/shard_map/pallas_call | solution.py:283
  76.8 4.2 %all-to-all-done.2.refs_0_ = bf16[16,448,128]{2,1,0:T(8,128)(2,1)S(1)} async-done(((bf16[16,448,128]{2,1,0:T(8,128)(2,1)}), bf16[16,448,128]{2,1,0:T(8,128)(2,1)S(1)}, u32[]{:S(2)}, u32[]{:S(2)}) %all-to-all-start.2) | async-done | bytes 1835040 | tf_op jit(solution)/shard_map/all_to_all | solution.py:354
  81.0 7.1 %all-to-all-start.4 = ((bf16[16,3,256,128]{3,2,1,0:T(8,128)(2,1)}), bf16[16,3,256,128]{3,2,1,0:T(8,128)(2,1)}, u32[]{:S(2)}, u32[]{:S(2)}) async-start(bf16[16,3,256,128]{3,2,1,0:T(8,128)(2,1)} %shard_map.112), calls=%async_computation.4 | async-start | bytes 6291456 | tf_op jit(solution)/shard_map/all_to_all | solution.py:354
  88.4 2.0 %collective-permute-start.10 = (bf16[16,96,128]{2,1,0:T(8,128)(2,1)S(1)}, bf16[16,96,128]{2,1,0:T(8,128)(2,1)S(1)}, u32[]{:S(2)}, u32[]{:S(2)}) collective-permute-start(bf16[16,96,128]{2,1,0:T(8,128)(2,1)S(1)} %slice.15), channel_id=1, source_target_pairs={{0,32},{16,48},{32,64},{48,80},{64,96},{80,112},{96,0},{112,16},{1... | collective-permute-start | bytes 1179656 | tf_op jit(solution)/shard_map/ppermute | solution.py:360
  91.4 6.6 %collective-permute-done.11.refs_3_ = bf16[16,96,128]{2,1,0:T(8,128)(2,1)S(1)} collective-permute-done((bf16[16,96,128]{2,1,0:T(8,128)(2,1)S(1)}, bf16[16,96,128]{2,1,0:T(8,128)(2,1)S(1)}, u32[]{:S(2)}, u32[]{:S(2)}) %collective-permute-start.11) | collective-permute-done | bytes 393248 | tf_op jit(solution)/shard_map/ppermute | solution.py:360
  98.0 1.3 collective-permute-done.10.refs_2_
  99.9 1.3 collective-permute-done.12.refs_4_
  101.2 20.9 %shard_map.113 = bf16[16,3,256,128]{3,2,1,0:T(8,128)(2,1)} custom-call(s32[256]{0:T(256)S(1)} %reshape.13.tiles_ref, s32[32]{0:T(128)S(1)} %copy-done, s32[32]{0:T(128)S(1)} %select_reduce_fusion.order_ref, s32[8]{0:T(128)S(1)} %and_select_fusion.1.source_ref, bf16[16,448,128]{2,1,0:T(8,128)(2,1)S(1)} %all-to-all-done.2.refs_0_, ...), custom_call_target="tpu_custom_call" | custom-call | flops 1000000 | bytes 1048576 | tf_op jit(solution)/shard_map/pallas_call | solution.py:283
  122.0 4.9 %all-to-all-done.4.src = bf16[16,3,256,128]{3,2,1,0:T(8,128)(2,1)} async-done(((bf16[16,3,256,128]{3,2,1,0:T(8,128)(2,1)}), bf16[16,3,256,128]{3,2,1,0:T(8,128)(2,1)}, u32[]{:S(2)}, u32[]{:S(2)}) %all-to-all-start.4) | async-done | bytes 3145760 | tf_op jit(solution)/shard_map/all_to_all | solution.py:354
  126.9 7.4 %all-to-all-start.3 = ((bf16[16,3,256,128]{3,2,1,0:T(8,128)(2,1)}), bf16[16,3,256,128]{3,2,1,0:T(8,128)(2,1)S(1)}, u32[]{:S(2)}, u32[]{:S(2)}) async-start(bf16[16,3,256,128]{3,2,1,0:T(8,128)(2,1)} %shard_map.113), calls=%async_computation.3 | async-start | bytes 6291456 | tf_op jit(solution)/shard_map/all_to_all | solution.py:354
  134.3 3.9 %shard_map.114 = (bf16[256,4096]{1,0:T(8,128)(2,1)}, bf16[256,4096]{1,0:T(8,128)(2,1)}, bf16[256,4096]{1,0:T(8,128)(2,1)}) custom-call(bf16[16,3,256,128]{3,2,1,0:T(8,128)(2,1)} %all-to-all-done.4.src), custom_call_target="tpu_custom_call" | custom-call | tf_op jit(solution)/shard_map/pallas_call | solution.py:335
  138.2 32.1 %all-to-all-done.3.src = bf16[16,3,256,128]{3,2,1,0:T(8,128)(2,1)S(1)} async-done(((bf16[16,3,256,128]{3,2,1,0:T(8,128)(2,1)}), bf16[16,3,256,128]{3,2,1,0:T(8,128)(2,1)S(1)}, u32[]{:S(2)}, u32[]{:S(2)}) %all-to-all-start.3) | async-done | bytes 3145760 | tf_op jit(solution)/shard_map/all_to_all | solution.py:354
  170.3 2.0 %shard_map.115 = (bf16[256,4096]{1,0:T(8,128)(2,1)}, bf16[256,4096]{1,0:T(8,128)(2,1)}, bf16[256,4096]{1,0:T(8,128)(2,1)}) custom-call(bf16[16,3,256,128]{3,2,1,0:T(8,128)(2,1)S(1)} %all-to-all-done.3.src, bf16[256,4096]{1,0:T(8,128)(2,1)} %get-tuple-element.23.refs_0_, ...), custom_call_target="tpu_custom_call", output_to_operand_aliasing={{0}: (1, {}), {1}: (2, {}), {2}: (3, {})} | custom-call | tf_op jit(solution)/shard_map/pallas_call | solution.py:335
  (37 shorter events, 5.6 us)
Async XLA Ops:
  2.6 15.4 %all-to-all-start = ((bf16[16,96,128]{2,1,0:T(8,128)(2,1)}), bf16[16,96,128]{2,1,0:T(8,128)(2,1)S(1)}, u32[]{:S(2)}, u32[]{:S(2)}) async-start(bf16[16,96,128]{2,1,0:T(8,128)(2,1)} %pack_first.1), calls=%async_computation | async-start | bytes 786432 | tf_op jit(solution)/shard_map/all_to_all | solution.py:354
  16.8 25.1 %copy-start = (s32[32]{0:T(128)S(1)}, s32[32]{0:T(128)}, u32[]{:S(2)}) copy-start(s32[32]{0:T(128)} %counts_ref.3) | copy-start | bytes 388
  16.8 25.3 %copy-start.1 = (s32[32,8]{0,1:T(8,128)S(1)}, s32[32,8]{0,1:T(8,128)}, u32[]{:S(2)}) copy-start(s32[32,8]{0,1:T(8,128)} %param.16) | copy-start | bytes 3076
  18.0 30.3 %all-to-all-start.1 = ((bf16[16,256,128]{2,1,0:T(8,128)(2,1)}), bf16[16,256,128]{2,1,0:T(8,128)(2,1)S(1)}, u32[]{:S(2)}, u32[]{:S(2)}) async-start(bf16[16,256,128]{2,1,0:T(8,128)(2,1)} %get-tuple-element.19), calls=%async_computation.1 | async-start | bytes 2097152 | tf_op jit(solution)/shard_map/all_to_all | solution.py:354
  24.3 11.2 %collective-permute-start.2 = (bf16[16,96,128]{2,1,0:T(8,128)(2,1)S(1)}, bf16[16,96,128]{2,1,0:T(8,128)(2,1)}, u32[]{:S(2)}, u32[]{:S(2)}) collective-permute-start(bf16[16,96,128]{2,1,0:T(8,128)(2,1)S(1)} %all-to-all-done.refs_0_), channel_id=1, source_target_pairs={{0,96},{16,112},{32,0},{48,16},{64,32},{80,48},{96,64},{112,80},{1... | collective-permute-start | bytes 1179656 | tf_op jit(solution)/shard_map/ppermute | solution.py:360
  28.2 12.1 %collective-permute-start.1 = (bf16[16,96,128]{2,1,0:T(8,128)(2,1)S(1)}, bf16[16,96,128]{2,1,0:T(8,128)(2,1)}, u32[]{:S(2)}, u32[]{:S(2)}) collective-permute-start(bf16[16,96,128]{2,1,0:T(8,128)(2,1)S(1)} %all-to-all-done.refs_0_), channel_id=1, source_target_pairs={{0,32},{16,48},{32,64},{48,80},{64,96},{80,112},{96,0},{112,16},{1... | collective-permute-start | bytes 1179656 | tf_op jit(solution)/shard_map/ppermute | solution.py:360
  28.2 27.3 %collective-permute-start = (bf16[16,96,128]{2,1,0:T(8,128)(2,1)S(1)}, bf16[16,96,128]{2,1,0:T(8,128)(2,1)}, u32[]{:S(2)}, u32[]{:S(2)}) collective-permute-start(bf16[16,96,128]{2,1,0:T(8,128)(2,1)S(1)} %all-to-all-done.refs_0_), channel_id=1, source_target_pairs={{0,16},{16,0},{32,48},{48,32},{64,80},{80,64},{96,112},{112,96},{1... | collective-permute-start | bytes 1179656 | tf_op jit(solution)/shard_map/ppermute | solution.py:363
  36.4 7.1 %collective-permute-start.6 = (bf16[8,96,128]{2,1,0:T(8,128)(2,1)S(1)}, bf16[8,96,128]{2,1,0:T(8,128)(2,1)}, u32[]{:S(2)}, u32[]{:S(2)}) collective-permute-start(bf16[8,96,128]{2,1,0:T(8,128)(2,1)S(1)} %slice.17), channel_id=1, source_target_pairs={{0,96},{16,112},{32,0},{48,16},{64,32},{80,48},{96,64},{112,80},{1... | collective-permute-start | bytes 589832 | tf_op jit(solution)/shard_map/ppermute | solution.py:360
  41.2 7.1 %collective-permute-start.5 = (bf16[8,96,128]{2,1,0:T(8,128)(2,1)S(1)}, bf16[8,96,128]{2,1,0:T(8,128)(2,1)}, u32[]{:S(2)}, u32[]{:S(2)}) collective-permute-start(bf16[8,96,128]{2,1,0:T(8,128)(2,1)S(1)} %slice.16), channel_id=1, source_target_pairs={{0,32},{16,48},{32,64},{48,80},{64,96},{80,112},{96,0},{112,16},{1... | collective-permute-start | bytes 589832 | tf_op jit(solution)/shard_map/ppermute | solution.py:360
  41.3 14.3 %collective-permute-start.4 = (bf16[16,96,128]{2,1,0:T(8,128)(2,1)}, bf16[16,96,128]{2,1,0:T(8,128)(2,1)}, u32[]{:S(2)}, u32[]{:S(2)}) collective-permute-start(bf16[16,96,128]{2,1,0:T(8,128)(2,1)} %collective-permute-done.2.refs_3_), channel_id=1, source_target_pairs={{0,16},{16,0},{32,48},{48,32},{64,80},{80,64},{96,112},{112,96},{1... | collective-permute-start | bytes 1179656 | tf_op jit(solution)/shard_map/ppermute | solution.py:363
  41.4 14.2 %collective-permute-start.3 = (bf16[16,96,128]{2,1,0:T(8,128)(2,1)}, bf16[16,96,128]{2,1,0:T(8,128)(2,1)}, u32[]{:S(2)}, u32[]{:S(2)}) collective-permute-start(bf16[16,96,128]{2,1,0:T(8,128)(2,1)} %collective-permute-done.1.refs_2_), channel_id=1, source_target_pairs={{0,16},{16,0},{32,48},{48,32},{64,80},{80,64},{96,112},{112,96},{1... | collective-permute-start | bytes 1179656 | tf_op jit(solution)/shard_map/ppermute | solution.py:363
  43.5 12.1 %collective-permute-start.8 = (bf16[8,96,128]{2,1,0:T(8,128)(2,1)}, bf16[8,96,128]{2,1,0:T(8,128)(2,1)}, u32[]{:S(2)}, u32[]{:S(2)}) collective-permute-start(bf16[8,96,128]{2,1,0:T(8,128)(2,1)} %collective-permute-done.6.refs_7_), channel_id=1, source_target_pairs={{0,16},{16,0},{32,48},{48,32},{64,80},{80,64},{96,112},{112,96},{1... | collective-permute-start | bytes 589832 | tf_op jit(solution)/shard_map/ppermute | solution.py:363
  48.3 7.3 %collective-permute-start.7 = (bf16[8,96,128]{2,1,0:T(8,128)(2,1)}, bf16[8,96,128]{2,1,0:T(8,128)(2,1)}, u32[]{:S(2)}, u32[]{:S(2)}) collective-permute-start(bf16[8,96,128]{2,1,0:T(8,128)(2,1)} %collective-permute-done.5.refs_6_), channel_id=1, source_target_pairs={{0,16},{16,0},{32,48},{48,32},{64,80},{80,64},{96,112},{112,96},{1... | collective-permute-start | bytes 589832 | tf_op jit(solution)/shard_map/ppermute | solution.py:363
  48.3 32.7 %all-to-all-start.2 = ((bf16[16,448,128]{2,1,0:T(8,128)(2,1)}), bf16[16,448,128]{2,1,0:T(8,128)(2,1)S(1)}, u32[]{:S(2)}, u32[]{:S(2)}) async-start(bf16[16,448,128]{2,1,0:T(8,128)(2,1)} %get-tuple-element.20), calls=%async_computation.2 | async-start | bytes 3670016 | tf_op jit(solution)/shard_map/all_to_all | solution.py:354
  81.0 45.9 %all-to-all-start.4 = ((bf16[16,3,256,128]{3,2,1,0:T(8,128)(2,1)}), bf16[16,3,256,128]{3,2,1,0:T(8,128)(2,1)}, u32[]{:S(2)}, u32[]{:S(2)}) async-start(bf16[16,3,256,128]{3,2,1,0:T(8,128)(2,1)} %shard_map.112), calls=%async_computation.4 | async-start | bytes 6291456 | tf_op jit(solution)/shard_map/all_to_all | solution.py:354
  88.2 9.8 %collective-permute-start.11 = (bf16[16,96,128]{2,1,0:T(8,128)(2,1)S(1)}, bf16[16,96,128]{2,1,0:T(8,128)(2,1)S(1)}, u32[]{:S(2)}, u32[]{:S(2)}) collective-permute-start(bf16[16,96,128]{2,1,0:T(8,128)(2,1)S(1)} %slice.15), channel_id=1, source_target_pairs={{0,96},{16,112},{32,0},{48,16},{64,32},{80,48},{96,64},{112,80},{1... | collective-permute-start | bytes 1179656 | tf_op jit(solution)/shard_map/ppermute | solution.py:360
  88.4 10.9 %collective-permute-start.10 = (bf16[16,96,128]{2,1,0:T(8,128)(2,1)S(1)}, bf16[16,96,128]{2,1,0:T(8,128)(2,1)S(1)}, u32[]{:S(2)}, u32[]{:S(2)}) collective-permute-start(bf16[16,96,128]{2,1,0:T(8,128)(2,1)S(1)} %slice.15), channel_id=1, source_target_pairs={{0,32},{16,48},{32,64},{48,80},{64,96},{80,112},{96,0},{112,16},{1... | collective-permute-start | bytes 1179656 | tf_op jit(solution)/shard_map/ppermute | solution.py:360
  91.4 9.8 %collective-permute-start.9 = (bf16[16,192,128]{2,1,0:T(8,128)(2,1)}, bf16[16,192,128]{2,1,0:T(8,128)(2,1)S(1)}, u32[]{:S(2)}, u32[]{:S(2)}) collective-permute-start(bf16[16,192,128]{2,1,0:T(8,128)(2,1)} %slice.14), channel_id=1, source_target_pairs={{0,16},{16,0},{32,48},{48,32},{64,80},{80,64},{96,112},{112,96},{1... | collective-permute-start | bytes 2359304 | tf_op jit(solution)/shard_map/ppermute | solution.py:363
  98.0 1.9 %collective-permute-start.13 = (bf16[16,96,128]{2,1,0:T(8,128)(2,1)S(1)}, bf16[16,96,128]{2,1,0:T(8,128)(2,1)}, u32[]{:S(2)}, u32[]{:S(2)}) collective-permute-start(bf16[16,96,128]{2,1,0:T(8,128)(2,1)S(1)} %collective-permute-done.11.refs_3_), channel_id=1, source_target_pairs={{0,16},{16,0},{32,48},{48,32},{64,80},{80,64},{96,112},{112,96},{1... | collective-permute-start | bytes 1179656 | tf_op jit(solution)/shard_map/ppermute | solution.py:363
  99.3 1.9 %collective-permute-start.12 = (bf16[16,96,128]{2,1,0:T(8,128)(2,1)S(1)}, bf16[16,96,128]{2,1,0:T(8,128)(2,1)}, u32[]{:S(2)}, u32[]{:S(2)}) collective-permute-start(bf16[16,96,128]{2,1,0:T(8,128)(2,1)S(1)} %collective-permute-done.10.refs_2_), channel_id=1, source_target_pairs={{0,16},{16,0},{32,48},{48,32},{64,80},{80,64},{96,112},{112,96},{1... | collective-permute-start | bytes 1179656 | tf_op jit(solution)/shard_map/ppermute | solution.py:363
  126.9 43.4 %all-to-all-start.3 = ((bf16[16,3,256,128]{3,2,1,0:T(8,128)(2,1)}), bf16[16,3,256,128]{3,2,1,0:T(8,128)(2,1)S(1)}, u32[]{:S(2)}, u32[]{:S(2)}) async-start(bf16[16,3,256,128]{3,2,1,0:T(8,128)(2,1)} %shard_map.113), calls=%async_computation.3 | async-start | bytes 6291456 | tf_op jit(solution)/shard_map/all_to_all | solution.py:354
